TPU v7x, 32 devices: a whole 2x2x4 slice. The times are simulated.
32 devices in a mesh: groups: 2 (over y), bank: 4 (over x, core), split: 4 (over z).
Axes of the slice: x: 2, y: 2, z: 4, core: 2. Of those that a mesh axis runs over, the one named last changes fastest.
Arguments:
- queries: bfloat16 [4096, 256], P(('groups', 'bank')), parts along dimension 0, may hold values from -48 to 48
- range_start: int32 [4096], P(('groups', 'bank')), parts along dimension 0, may hold values from 0 to 24574, as said below
- range_end: int32 [4096], P(('groups', 'bank')), parts along dimension 0, may hold values from 2 to 24576
- keys: bfloat16 [49152, 256], P(('groups', 'bank', 'split')), parts along dimension 0, may hold values from -4.5 to 4.5
- values: bfloat16 [49152, 256], P(('groups', 'bank', 'split')), parts along dimension 0, may hold values from -6 to 6
- floor_index: int32 [32], P(('groups', 'bank', 'split')), parts along dimension 0, may hold values from 0 to 7
- block_order: int32 [8], P('groups'), parts along dimension 0, may hold values from 0 to 3, each once
Outputs:
- retrieved: float32 [4096, 256], P(('groups', 'bank')), parts along dimension 0
- log_total: float32 [4096], P(('groups', 'bank')), parts along dimension 0
There are 2 independent parts, one for each index of `groups`. A program takes and returns all parts, laid end to end along the dimension named above; each array names one. Nothing has to cross between parts.
Inputs may be any that keep to these rules, and one draw needn't show every extreme that they name: range_start < range_end for every query, every range holds 2 or more items; query 0 covers all 24576 items, query 2048 - 2 covers items 0 and 1 only, and query 2048 - 1 covers the last two items only.
All inputs are finite; a program needn't handle non-finite values.
Results may differ from a plain program's by a relative error of at most 0.0015.
Values may be sent and summed in bfloat16 or wider, within the bound.
No kernel may reach another device: no remote copies, remote signals or barrier semaphores. Data moves between devices by JAX's collectives and lax.ppermute only.
A program may use at most 64 MiB of HBM per device.

v0:
```python
import functools
import math

import jax
import jax.numpy as jnp
from jax import lax
from jax.experimental import pallas as pl
from jax.experimental.pallas import tpu as pltpu
from jax.sharding import PartitionSpec as P

NEG = -1e30
LOW = -1e29
EMPTY = -16000.0
LOG2E = math.log2(math.e)
LN2 = math.log(2.0)
FAR = 1 << 28
MIN32 = -(1 << 31)
LANES = 128
STATS = 16
TOP = 32700.0
TILE_ITEMS = 1536
VMEM = pl.BlockSpec(memory_space=pltpu.VMEM)
SMEM = pl.BlockSpec(memory_space=pltpu.SMEM)
ANY = pl.BlockSpec(memory_space=pl.ANY)


def resident(a):
    return pltpu.with_memory_space_constraint(a, pltpu.VMEM)


def pack(pooled, lse):
    width, lanes = pooled.shape
    largest = jnp.maximum(jnp.max(jnp.abs(pooled), axis=0, keepdims=True), 1e-30)
    power = jnp.ceil(128.0 * jnp.log2(largest))
    coded = jnp.floor(pooled * (TOP * jnp.exp2(power * (-1.0 / 128.0))) + 0.5)
    high = jnp.floor(lse * 2.0 + 0.5)
    low = jnp.floor((lse - high * 0.5) * 65536.0 + 0.5)
    row = lax.broadcasted_iota(jnp.int32, (STATS, lanes), 0)
    stats = jnp.where(row == 0, power, jnp.where(row == 1, high, jnp.where(row == 2, low, 0.0)))
    return coded.astype(jnp.int32).astype(jnp.int16), stats.astype(jnp.int32).astype(jnp.int16)


def unpack_stats(stats):
    stats = stats.astype(jnp.int32).astype(jnp.float32)
    scale = jnp.exp2(stats[0:1] * (1.0 / 128.0)) * (1.0 / TOP)
    return scale, stats[1:2] * 0.5 + stats[2:3] * (1.0 / 65536.0)


def as_f32(coded):
    return coded.astype(jnp.int32).astype(jnp.float32)


def joined(parts, width):
    stats = [unpack_stats(load(width, STATS)) for load in parts]
    top = functools.reduce(jnp.maximum, [lse for _, lse in stats])
    weights = [jnp.exp2(lse - top) for _, lse in stats]
    total = functools.reduce(jnp.add, weights)
    inverse = 1.0 / total
    pooled = None
    for load, (scale, _), weight in zip(parts, stats, weights):
        term = as_f32(load(0, width)) * (weight * scale * inverse)
        pooled = term if pooled is None else pooled + term
    return pack(pooled, top + jnp.log2(total))


def flash_kernel(*refs, tile, chunk, scale, n_before):
    refs = list(refs)
    take = lambda count: [refs.pop(0) for _ in range(count)]
    query_ref, range_ref = take(2)
    sources = [take(3) for _ in range(2)]
    take(1)
    before = take(n_before or 0)
    score_ref, acc, *coded_refs = refs[-3:] if n_before is not None else (refs[-2], refs[-1], refs[0])
    outs = refs[:-3] if n_before is not None else []
    coded_ref = coded_refs[0]
    n, width = sources[0][1].shape
    rows = query_ref.shape[0]
    lanes = score_ref.shape[1]
    n_split = lax.axis_size("split")
    bank, split = lax.axis_index("bank"), lax.axis_index("split")
    sub = lax.broadcasted_iota(jnp.int32, (8, lanes), 0)

    @pl.loop(0, rows // lanes)
    def _(half):
        across = pl.ds(pl.multiple_of(half * lanes, lanes), lanes)
        query = query_ref[across, :]
        start, end = range_ref[0:1, across], range_ref[1:2, across]
        lowest, highest = jnp.min(start), jnp.max(end)
        length = (end - start) + jnp.int32(MIN32)
        peak = jnp.full((1, lanes), LOW, jnp.float32)
        bounds = []
        for number, (floor_ref, key_ref, _) in enumerate(sources):
            first = (jnp.bitwise_xor(bank, number) * n_split + split) * n
            floor = floor_ref[0].astype(jnp.float32) * (0.5 * LOG2E) - 2.0 * LOG2E
            begin = jnp.minimum(lax.div(jnp.maximum(lowest - first, 0), tile), n // tile)
            stop = jnp.minimum(lax.div(jnp.maximum(highest - first, 0) + (tile - 1), tile), n // tile)
            bounds.append((begin, stop))

            def score(t, peak, key_ref=key_ref, first=first, floor=floor, number=number):
                offset = pl.multiple_of(t * tile, tile)
                s = lax.dot_general(
                    key_ref[pl.ds(offset, tile), :], query, (((1,), (1,)), ((), ())),
                    preferred_element_type=jnp.float32,
                )
                s = jnp.maximum(s * (scale * LOG2E), floor).reshape(tile // 8, 8, lanes)
                from_start = sub + (first + offset - start) + jnp.int32(MIN32)
                parts = []
                for r in range(tile // 8):
                    x = jnp.where(from_start + 8 * r < length, s[r], NEG)
                    score_ref[pl.ds(number * n + offset + 8 * r, 8), :] = x
                    parts.append(x)
                while len(parts) > 1:
                    parts = [jnp.maximum(a, b) for a, b in zip(parts[::2], parts[1::2])] + parts[len(parts) // 2 * 2:]
                return jnp.maximum(peak, jnp.max(parts[0], axis=0, keepdims=True))

            peak = lax.fori_loop(begin, stop, score, peak)
        acc[...] = jnp.zeros_like(acc)
        mass = jnp.zeros((8, lanes), jnp.float32)
        for number, (_, _, value_ref) in enumerate(sources):

            def fold(t, mass, value_ref=value_ref, number=number):
                offset = pl.multiple_of(t * tile, tile)
                low = []
                for c in range(0, tile, chunk):
                    weight = jnp.exp2(score_ref[pl.ds(number * n + offset + c, chunk), :] - peak)
                    mass = mass + jnp.sum(weight.reshape(chunk // 8, 8, lanes), axis=0)
                    low.append(weight.astype(jnp.bfloat16))
                acc[...] += lax.dot_general(
                    value_ref[pl.ds(offset, tile), :], jnp.concatenate(low), (((0,), (0,)), ((), ())),
                    preferred_element_type=jnp.float32,
                )
                return mass

            mass = lax.fori_loop(*bounds[number], fold, mass)
        mass = jnp.sum(mass, axis=0, keepdims=True)
        safe = jnp.maximum(mass, 1.0)
        lse = jnp.where(mass > 0, peak + jnp.log2(safe), EMPTY)
        coded, stats = pack(acc[...] * (1.0 / safe), lse)
        for u in range(lanes // LANES):
            coded_ref[half * (lanes // LANES) + u, :width, :] = coded[:, u * LANES:(u + 1) * LANES]
            coded_ref[half * (lanes // LANES) + u, width:, :] = stats[:, u * LANES:(u + 1) * LANES]

    for k, out in enumerate(outs):
        per = out.shape[2]
        shares = LANES // per
        to = jnp.bitwise_xor(split, k)
        for g, source in enumerate([*before, coded_ref]):
            if shares == 1:
                out[g] = source[to]
                continue
            whole = source[lax.div(to, shares)].astype(jnp.int32)
            for u in range(shares):
                @pl.when(lax.rem(to, shares) == u)
                def _():
                    out[g] = whole[:, u * per:(u + 1) * per].astype(jnp.int16)


def flash(query, ranges, sources, after, before, scale, n_split):
    n, width = sources[0][1].shape
    rows = query.shape[0]
    lanes = min(256, rows)
    tile = TILE_ITEMS if n % TILE_ITEMS == 0 else 128
    coded = pltpu.VMEM((rows // LANES, width + STATS, LANES), jnp.int16)
    scratch = [pltpu.VMEM((2 * n, lanes), jnp.float32), pltpu.VMEM((width, lanes), jnp.float32)]
    out_shape = coded
    if before is not None:
        out_shape = [pltpu.VMEM((len(before) + 1, width + STATS, rows // n_split), jnp.int16)] * n_split
        scratch.append(coded)
    return pl.pallas_call(
        functools.partial(
            flash_kernel, tile=tile, chunk=min(tile, 256), scale=scale,
            n_before=None if before is None else len(before),
        ),
        out_shape=out_shape,
        in_specs=[VMEM] * 2 + [SMEM, VMEM, VMEM] * 2 + [ANY] + [VMEM] * len(before or ()),
        out_specs=VMEM if before is None else [VMEM] * n_split,
        scratch_shapes=scratch,
        compiler_params=pltpu.CompilerParams(vmem_limit_bytes=16 << 20),
        name="flash",
    )(
        resident(query), resident(ranges), *[b for f, k, v in sources for b in (f, resident(k), resident(v))], after,
        *map(resident, before or ()),
    )


def spread_kernel(order, *refs, n_bank, width):
    refs = list(refs)
    scratch = refs.pop()
    n_groups = scratch.shape[0] - 1
    parts, outs = refs[:-n_bank], refs[-n_bank:]
    bank = lax.axis_index("bank")
    lanes = scratch.shape[2]
    for g in range(n_groups):
        coded, stats = joined([lambda at, size, part=part: part[g, at:at + size, :] for part in parts], width)
        scratch[g, :width, :] = coded
        scratch[g, width:, :] = stats
    row = lax.broadcasted_iota(jnp.int32, (STATS, lanes), 0)
    scratch[n_groups, :width, :] = jnp.zeros((width, lanes), jnp.int16)
    scratch[n_groups, width:, :] = jnp.where(row == 1, 2.0 * EMPTY, 0.0).astype(jnp.int32).astype(jnp.int16)
    for m, out in enumerate(outs):
        block = order[jnp.bitwise_xor(bank, m)]
        which = jnp.int32(n_groups)
        for g in range(n_groups):
            which = jnp.where(block == jnp.bitwise_xor(bank, 2 * g), g, which)
        out[...] = scratch[which]


def gather_kernel(*refs, width):
    *parts, out = refs
    coded, stats = joined([lambda at, size, part=part: part[at:at + size, :] for part in parts], width)
    out[:width, :] = coded
    out[width:, :] = stats


def final_kernel(*refs, width):
    *parts, retrieved, log_total = refs
    lanes = parts[0].shape[1]
    for k, part in enumerate(parts):
        at = jnp.bitwise_xor(lax.axis_index("split"), k)
        scale, lse = unpack_stats(part[width:, :])
        retrieved[pl.ds(pl.multiple_of(at * lanes, lanes), lanes), :] = (as_f32(part[:width, :]) * scale).T
        log_total[pl.ds(at, 1), :] = lse * LN2


def local(queries, range_start, range_end, keys, values, floor_index, block_order):
    n_bank = lax.axis_size("bank")
    n_split = lax.axis_size("split")
    width = keys.shape[1]
    block_rows = queries.shape[0]
    per = block_rows // n_split
    scale = 2.0 / math.sqrt(width)

    def over(axis, mask):
        size = lax.axis_size(axis)
        return lambda a: lax.ppermute(a, axis, [(i, i ^ mask) for i in range(size)])

    ranges = jnp.stack([range_start, range_end])
    own = (floor_index, keys, values)
    partner = tuple(over("bank", 1)(a) for a in own)
    asked = [(over("bank", 2 * g)(queries), over("bank", 2 * g)(ranges)) for g in range(1, n_bank // 2)]
    coded = []
    for number, (q, r) in enumerate([(queries, ranges)] + asked):
        before = coded if number == len(asked) else None
        result = flash(q, r, [own, partner], asked[0][1], before, scale, n_split)
        coded.append(result)
    messages = coded[-1]
    parts = [messages[0]] + [over("split", k)(messages[k]) for k in range(1, n_split)]
    packed = pltpu.VMEM((width + STATS, per), jnp.int16)
    spread = pl.pallas_call(
        functools.partial(spread_kernel, n_bank=n_bank, width=width),
        out_shape=[packed] * n_bank,
        in_specs=[SMEM] + [VMEM] * n_split,
        out_specs=[VMEM] * n_bank,
        scratch_shapes=[pltpu.VMEM((len(coded) + 1, width + STATS, per), jnp.int16)],
        compiler_params=pltpu.CompilerParams(vmem_limit_bytes=16 << 20),
        name="spread",
    )(block_order, *map(resident, parts))
    parts = [spread[0]] + [over("bank", m)(spread[m]) for m in range(1, n_bank)]
    own = pl.pallas_call(
        functools.partial(gather_kernel, width=width),
        out_shape=packed,
        in_specs=[VMEM] * n_bank,
        out_specs=VMEM,
        compiler_params=pltpu.CompilerParams(vmem_limit_bytes=16 << 20),
        name="gather",
    )(*map(resident, parts))
    parts = [own] + [over("split", k)(own) for k in range(1, n_split)]
    retrieved, log_total = pl.pallas_call(
        functools.partial(final_kernel, width=width),
        out_shape=(
            jax.ShapeDtypeStruct((block_rows, width), jnp.float32),
            jax.ShapeDtypeStruct((n_split, per), jnp.float32),
        ),
        in_specs=[VMEM] * n_split,
        out_specs=(VMEM, VMEM),
        compiler_params=pltpu.CompilerParams(vmem_limit_bytes=16 << 20),
        name="final",
    )(*map(resident, parts))
    return retrieved, log_total.reshape(block_rows)


def solution(mesh):
    in_specs = (
        P(("groups", "bank"), None),
        P(("groups", "bank")),
        P(("groups", "bank")),
        P(("groups", "bank", "split"), None),
        P(("groups", "bank", "split"), None),
        P(("groups", "bank", "split")),
        P("groups"),
    )
    out_specs = (P(("groups", "bank"), None), P(("groups", "bank")))
    return jax.shard_map(local, mesh=mesh, in_specs=in_specs, out_specs=out_specs, check_vma=False)
```

profile of v0, /device:TPU:0, one launch (start us, length us, event | category | flops | bytes accessed | tf_op | source)
XLA Modules:
  0.0 57.5 jit_solution(16252340830833128199)
XLA Ops:
  0.6 0.0 copy-start.6
  0.6 0.6 collective-permute-start.3
  1.2 0.1 collective-permute-start.4
  1.3 2.9 %collective-permute-start = (bf16[512,256]{1,0:T(8,128)(2,1)}, bf16[512,256]{1,0:T(8,128)(2,1)S(1)}, u32[]{:S(2)}, u32[]{:S(2)}) collective-permute-start(bf16[512,256]{1,0:T(8,128)(2,1)} %refs_0_.1), channel_id=1, source_target_pairs={{0,8},{4,12},{8,0},{12,4},{1,9},{5,13},{9,1},{13,5},{2,10},{6,14},... | collective-permute-start | bytes 786440 | tf_op jit(solution)/shard_map/ppermute | solution.py:235
  4.2 0.0 copy-done.6
  4.2 0.7 %pad_add_fusion.refs_1_ = s32[2,512]{1,0:T(2,128)S(1)} fusion(s32[1,512]{1,0:T(1,128)S(1)} %bitcast.3, s32[1,512]{1,0:T(1,128)} %bitcast.4), kind=kLoop, calls=%fused_computation | loop fusion | flops 1024 | bytes 8192 | tf_op jit(solution)/shard_map/stack | solution.py:237
  4.9 0.1 collective-permute-start.1
  5.0 0.0 collective-permute-start.2
  5.6 0.6 %collective-permute-done.2.refs_5_ = s32[1]{0:T(128)} collective-permute-done((s32[1]{0:T(128)}, s32[1]{0:T(128)}, u32[]{:S(2)}, u32[]{:S(2)}) %collective-permute-start.2) | collective-permute-done | bytes 36 | tf_op jit(solution)/shard_map/ppermute | solution.py:235
  6.2 4.8 %collective-permute-done.1.refs_8_.refs_1_ = s32[2,512]{1,0:T(2,128)S(1)} collective-permute-done((s32[2,512]{1,0:T(2,128)S(1)}, s32[2,512]{1,0:T(2,128)S(1)}, u32[]{:S(2)}, u32[]{:S(2)}) %collective-permute-start.1) | collective-permute-done | bytes 4128 | tf_op jit(solution)/shard_map/ppermute | solution.py:235
  11.0 0.0 collective-permute-done.3.refs_6_
  11.0 0.0 collective-permute-done.4.refs_7_
  11.0 0.0 copy-start
  11.0 1.1 %copy-done = bf16[1536,256]{1,0:T(8,128)(2,1)S(1)} copy-done((bf16[1536,256]{1,0:T(8,128)(2,1)S(1)}, bf16[1536,256]{1,0:T(8,128)(2,1)}, u32[]{:S(2)}) %copy-start) | copy-done | bytes 786456
  12.2 0.0 copy-start.2
  12.2 1.1 %copy-done.2 = bf16[1536,256]{1,0:T(8,128)(2,1)S(1)} copy-done((bf16[1536,256]{1,0:T(8,128)(2,1)S(1)}, bf16[1536,256]{1,0:T(8,128)(2,1)}, u32[]{:S(2)}) %copy-start.2) | copy-done | bytes 786456
  13.3 0.0 copy-start.4
  13.3 0.9 %copy-done.4 = bf16[512,256]{1,0:T(8,128)(2,1)S(1)} copy-done((bf16[512,256]{1,0:T(8,128)(2,1)S(1)}, bf16[512,256]{1,0:T(8,128)(2,1)}, u32[]{:S(2)}) %copy-start.4) | copy-done | bytes 262168
  14.3 0.0 copy-start.1
  14.3 0.0 copy-start.3
  14.3 3.6 %flash.2.refs_9_ = s16[4,272,128]{2,1,0:T(8,128)(2,1)S(1)} custom-call(bf16[512,256]{1,0:T(8,128)(2,1)S(1)} %copy-done.4, s32[2,512]{1,0:T(2,128)S(1)} %pad_add_fusion.refs_1_, s32[1]{0:T(128)S(6)} %copy.9.refs_2_, bf16[1536,256]{1,0:T(8,128)(2,1)S(1)} %copy-done, bf16[1536,256]{1,0:T(8,128)(2,1)S(1)} %copy-done.2, s32[1]{0:T(128)} %collective-permute-done.2.refs_5_, ...), custom_call_target="tpu_custom_call" | custom-call | tf_op jit(solution)/shard_map/flash/pallas_call | solution.py:169
  17.9 0.0 collective-permute-done.refs_0_
  17.9 0.0 copy-done.1
  17.9 0.0 copy-done.3
  17.9 5.6 %flash.3 = (s16[2,272,128]{2,1,0:T(8,128)(2,1)S(1)}, s16[2,272,128]{2,1,0:T(8,128)(2,1)S(1)}, s16[2,272,128]{2,1,0:T(8,128)(2,1)S(1)}, s16[2,272,128]{2,1,0:T(8,128)(2,1)S(1)}) custom-call(bf16[512,256]{1,0:T(8,128)(2,1)S(1)} %collective-permute-done.refs_0_, s32[2,512]{1,0:T(2,128)S(1)} %collective-permute-done.1.refs_8_.refs_1_, s32[1]{0:T(128)S(6)} %copy.9.refs_2_, ...), custom_call_target="tpu_custom_call" | custom-call | tf_op jit(solution)/shard_map/flash/pallas_call | solution.py:169
  23.5 1.9 %collective-permute-start.5 = (s16[2,272,128]{2,1,0:T(8,128)(2,1)S(1)}, s16[2,272,128]{2,1,0:T(8,128)(2,1)S(1)}, u32[]{:S(2)}, u32[]{:S(2)}) collective-permute-start(s16[2,272,128]{2,1,0:T(8,128)(2,1)S(1)} %get-tuple-element.13), channel_id=1, source_target_pairs={{0,1},{1,0},{2,3},{3,2},{4,5},{5,4},{6,7},{7,6},{8,9},{9,8},{10,11... | collective-permute-start | bytes 417800 | tf_op jit(solution)/shard_map/ppermute | solution.py:235
  25.4 3.7 %collective-permute-start.6 = (s16[2,272,128]{2,1,0:T(8,128)(2,1)S(1)}, s16[2,272,128]{2,1,0:T(8,128)(2,1)S(1)}, u32[]{:S(2)}, u32[]{:S(2)}) collective-permute-start(s16[2,272,128]{2,1,0:T(8,128)(2,1)S(1)} %get-tuple-element.14), channel_id=1, source_target_pairs={{0,2},{1,3},{2,0},{3,1},{4,6},{5,7},{6,4},{7,5},{8,10},{9,11},{10,... | collective-permute-start | bytes 417800 | tf_op jit(solution)/shard_map/ppermute | solution.py:235
  29.1 0.0 copy-start.5
  29.1 0.0 collective-permute-start.7
  29.1 2.3 %collective-permute-done.5.refs_1_ = s16[2,272,128]{2,1,0:T(8,128)(2,1)S(1)} collective-permute-done((s16[2,272,128]{2,1,0:T(8,128)(2,1)S(1)}, s16[2,272,128]{2,1,0:T(8,128)(2,1)S(1)}, u32[]{:S(2)}, u32[]{:S(2)}) %collective-permute-start.5) | collective-permute-done | bytes 139296 | tf_op jit(solution)/shard_map/ppermute | solution.py:235
  31.4 8.0 %collective-permute-done.6.refs_2_ = s16[2,272,128]{2,1,0:T(8,128)(2,1)S(1)} collective-permute-done((s16[2,272,128]{2,1,0:T(8,128)(2,1)S(1)}, s16[2,272,128]{2,1,0:T(8,128)(2,1)S(1)}, u32[]{:S(2)}, u32[]{:S(2)}) %collective-permute-start.6) | collective-permute-done | bytes 139296 | tf_op jit(solution)/shard_map/ppermute | solution.py:235
  39.4 0.0 collective-permute-done.7.refs_3_
  39.4 0.0 copy-done.5
  39.4 0.8 %spread.1 = (s16[272,128]{1,0:T(8,128)(2,1)S(1)}, s16[272,128]{1,0:T(8,128)(2,1)S(1)}, s16[272,128]{1,0:T(8,128)(2,1)S(1)}, s16[272,128]{1,0:T(8,128)(2,1)S(1)}) custom-call(s32[4]{0:T(128)S(1)} %copy-done.5, s16[2,272,128]{2,1,0:T(8,128)(2,1)S(1)} %get-tuple-element.12.refs_0_, s16[2,272,128]{2,1,0:T(8,128)(2,1)S(1)} %collective-permute-done.5.refs_1_, ...), custom_call_target="tpu_custom_call" | custom-call | tf_op jit(solution)/shard_map/spread/pallas_call | solution.py:249
  40.2 0.1 collective-permute-start.8
  40.3 0.1 collective-permute-start.9
  40.4 1.8 %collective-permute-start.10 = (s16[272,128]{1,0:T(8,128)(2,1)S(1)}, s16[272,128]{1,0:T(8,128)(2,1)S(1)}, u32[]{:S(2)}, u32[]{:S(2)}) collective-permute-start(s16[272,128]{1,0:T(8,128)(2,1)S(1)} %get-tuple-element.19), channel_id=1, source_target_pairs={{0,12},{4,8},{8,4},{12,0},{1,13},{5,9},{9,5},{13,1},{2,14},{6,10},... | collective-permute-start | bytes 208904 | tf_op jit(solution)/shard_map/ppermute | solution.py:235
  42.1 0.0 collective-permute-done.8.refs_1_
  42.1 3.3 %collective-permute-done.9.refs_2_ = s16[272,128]{1,0:T(8,128)(2,1)S(1)} collective-permute-done((s16[272,128]{1,0:T(8,128)(2,1)S(1)}, s16[272,128]{1,0:T(8,128)(2,1)S(1)}, u32[]{:S(2)}, u32[]{:S(2)}) %collective-permute-start.9) | collective-permute-done | bytes 69664 | tf_op jit(solution)/shard_map/ppermute | solution.py:235
  45.4 0.4 collective-permute-done.10.refs_3_
  45.8 0.1 gather.1.refs_0_
  46.0 2.4 %collective-permute-start.13 = (s16[272,128]{1,0:T(8,128)(2,1)S(1)}, s16[272,128]{1,0:T(8,128)(2,1)S(1)}, u32[]{:S(2)}, u32[]{:S(2)}) collective-permute-start(s16[272,128]{1,0:T(8,128)(2,1)S(1)} %gather.1.refs_0_), channel_id=1, source_target_pairs={{0,3},{1,2},{2,1},{3,0},{4,7},{5,6},{6,5},{7,4},{8,11},{9,10},{10,... | collective-permute-start | bytes 208904 | tf_op jit(solution)/shard_map/ppermute | solution.py:235
  48.3 1.2 %collective-permute-start.12 = (s16[272,128]{1,0:T(8,128)(2,1)S(1)}, s16[272,128]{1,0:T(8,128)(2,1)S(1)}, u32[]{:S(2)}, u32[]{:S(2)}) collective-permute-start(s16[272,128]{1,0:T(8,128)(2,1)S(1)} %gather.1.refs_0_), channel_id=1, source_target_pairs={{0,2},{1,3},{2,0},{3,1},{4,6},{5,7},{6,4},{7,5},{8,10},{9,11},{10,... | collective-permute-start | bytes 208904 | tf_op jit(solution)/shard_map/ppermute | solution.py:235
  49.5 0.9 %collective-permute-start.11 = (s16[272,128]{1,0:T(8,128)(2,1)S(1)}, s16[272,128]{1,0:T(8,128)(2,1)S(1)}, u32[]{:S(2)}, u32[]{:S(2)}) collective-permute-start(s16[272,128]{1,0:T(8,128)(2,1)S(1)} %gather.1.refs_0_), channel_id=1, source_target_pairs={{0,1},{1,0},{2,3},{3,2},{4,5},{5,4},{6,7},{7,6},{8,9},{9,8},{10,11... | collective-permute-start | bytes 208904 | tf_op jit(solution)/shard_map/ppermute | solution.py:235
  50.4 2.0 %collective-permute-done.13.refs_3_ = s16[272,128]{1,0:T(8,128)(2,1)S(1)} collective-permute-done((s16[272,128]{1,0:T(8,128)(2,1)S(1)}, s16[272,128]{1,0:T(8,128)(2,1)S(1)}, u32[]{:S(2)}, u32[]{:S(2)}) %collective-permute-start.13) | collective-permute-done | bytes 69664 | tf_op jit(solution)/shard_map/ppermute | solution.py:235
  52.4 4.0 %collective-permute-done.12.refs_2_ = s16[272,128]{1,0:T(8,128)(2,1)S(1)} collective-permute-done((s16[272,128]{1,0:T(8,128)(2,1)S(1)}, s16[272,128]{1,0:T(8,128)(2,1)S(1)}, u32[]{:S(2)}, u32[]{:S(2)}) %collective-permute-start.12) | collective-permute-done | bytes 69664 | tf_op jit(solution)/shard_map/ppermute | solution.py:235
  56.4 0.0 collective-permute-done.11.refs_1_
  56.4 1.0 %final.1 = (f32[512,256]{1,0:T(8,128)}, f32[4,128]{1,0:T(4,128)}) custom-call(s16[272,128]{1,0:T(8,128)(2,1)S(1)} %gather.1.refs_0_, s16[272,128]{1,0:T(8,128)(2,1)S(1)} %collective-permute-done.11.refs_1_, s16[272,128]{1,0:T(8,128)(2,1)S(1)} %collective-permute-done.12.refs_2_, s16[272,128]{1,0:T(8,128)(2,1)S(1)} %collective-permute-done.13.refs_3_), custom_call_target="tpu_custom_call" | custom-call | tf_op jit(solution)/shard_map/final/pallas_call | solution.py:268
Async XLA Ops:
  0.6 3.6 %copy-start.6 = (s32[512]{0:T(512)S(1)}, s32[512]{0:T(512)}, u32[]{:S(2)}) copy-start(s32[512]{0:T(512)} %param.9) | copy-start | bytes 6148
  0.6 10.4 %collective-permute-start.3 = (bf16[1536,256]{1,0:T(8,128)(2,1)}, bf16[1536,256]{1,0:T(8,128)(2,1)S(1)}, u32[]{:S(2)}, u32[]{:S(2)}) collective-permute-start(bf16[1536,256]{1,0:T(8,128)(2,1)} %refs_3_.3), channel_id=1, source_target_pairs={{0,4},{4,0},{8,12},{12,8},{1,5},{5,1},{9,13},{13,9},{2,6},{6,2},{1... | collective-permute-start | bytes 2359304 | tf_op jit(solution)/shard_map/ppermute | solution.py:235
  1.2 9.8 %collective-permute-start.4 = (bf16[1536,256]{1,0:T(8,128)(2,1)}, bf16[1536,256]{1,0:T(8,128)(2,1)S(1)}, u32[]{:S(2)}, u32[]{:S(2)}) collective-permute-start(bf16[1536,256]{1,0:T(8,128)(2,1)} %refs_4_.3), channel_id=1, source_target_pairs={{0,4},{4,0},{8,12},{12,8},{1,5},{5,1},{9,13},{13,9},{2,6},{6,2},{1... | collective-permute-start | bytes 2359304 | tf_op jit(solution)/shard_map/ppermute | solution.py:235
  1.3 16.6 %collective-permute-start = (bf16[512,256]{1,0:T(8,128)(2,1)}, bf16[512,256]{1,0:T(8,128)(2,1)S(1)}, u32[]{:S(2)}, u32[]{:S(2)}) collective-permute-start(bf16[512,256]{1,0:T(8,128)(2,1)} %refs_0_.1), channel_id=1, source_target_pairs={{0,8},{4,12},{8,0},{12,4},{1,9},{5,13},{9,1},{13,5},{2,10},{6,14},... | collective-permute-start | bytes 786440 | tf_op jit(solution)/shard_map/ppermute | solution.py:235
  4.9 6.2 %collective-permute-start.1 = (s32[2,512]{1,0:T(2,128)S(1)}, s32[2,512]{1,0:T(2,128)S(1)}, u32[]{:S(2)}, u32[]{:S(2)}) collective-permute-start(s32[2,512]{1,0:T(2,128)S(1)} %pad_add_fusion.refs_1_), channel_id=1, source_target_pairs={{0,8},{4,12},{8,0},{12,4},{1,9},{5,13},{9,1},{13,5},{2,10},{6,14},... | collective-permute-start | bytes 12296 | tf_op jit(solution)/shard_map/ppermute | solution.py:235
  5.0 1.3 %collective-permute-start.2 = (s32[1]{0:T(128)}, s32[1]{0:T(128)}, u32[]{:S(2)}, u32[]{:S(2)}) collective-permute-start(s32[1]{0:T(128)} %param.12), channel_id=1, source_target_pairs={{0,4},{4,0},{8,12},{12,8},{1,5},{5,1},{9,13},{13,9},{2,6},{6,2},{1... | collective-permute-start | bytes 20 | tf_op jit(solution)/shard_map/ppermute | solution.py:235
  11.0 1.1 %copy-start = (bf16[1536,256]{1,0:T(8,128)(2,1)S(1)}, bf16[1536,256]{1,0:T(8,128)(2,1)}, u32[]{:S(2)}) copy-start(bf16[1536,256]{1,0:T(8,128)(2,1)} %refs_3_.3) | copy-start | bytes 2359300
  12.2 1.1 %copy-start.2 = (bf16[1536,256]{1,0:T(8,128)(2,1)S(1)}, bf16[1536,256]{1,0:T(8,128)(2,1)}, u32[]{:S(2)}) copy-start(bf16[1536,256]{1,0:T(8,128)(2,1)} %refs_4_.3) | copy-start | bytes 2359300
  13.3 0.9 %copy-start.4 = (bf16[512,256]{1,0:T(8,128)(2,1)S(1)}, bf16[512,256]{1,0:T(8,128)(2,1)}, u32[]{:S(2)}) copy-start(bf16[512,256]{1,0:T(8,128)(2,1)} %refs_0_.1) | copy-start | bytes 786436
  14.3 3.6 %copy-start.1 = (bf16[1536,256]{1,0:T(8,128)(2,1)S(1)}, bf16[1536,256]{1,0:T(8,128)(2,1)}, u32[]{:S(2)}) copy-start(bf16[1536,256]{1,0:T(8,128)(2,1)} %refs_3_.3) | copy-start | bytes 2359300
  14.3 3.6 %copy-start.3 = (bf16[1536,256]{1,0:T(8,128)(2,1)S(1)}, bf16[1536,256]{1,0:T(8,128)(2,1)}, u32[]{:S(2)}) copy-start(bf16[1536,256]{1,0:T(8,128)(2,1)} %refs_4_.3) | copy-start | bytes 2359300
  23.5 7.9 %collective-permute-start.5 = (s16[2,272,128]{2,1,0:T(8,128)(2,1)S(1)}, s16[2,272,128]{2,1,0:T(8,128)(2,1)S(1)}, u32[]{:S(2)}, u32[]{:S(2)}) collective-permute-start(s16[2,272,128]{2,1,0:T(8,128)(2,1)S(1)} %get-tuple-element.13), channel_id=1, source_target_pairs={{0,1},{1,0},{2,3},{3,2},{4,5},{5,4},{6,7},{7,6},{8,9},{9,8},{10,11... | collective-permute-start | bytes 417800 | tf_op jit(solution)/shard_map/ppermute | solution.py:235
  25.4 14.0 %collective-permute-start.6 = (s16[2,272,128]{2,1,0:T(8,128)(2,1)S(1)}, s16[2,272,128]{2,1,0:T(8,128)(2,1)S(1)}, u32[]{:S(2)}, u32[]{:S(2)}) collective-permute-start(s16[2,272,128]{2,1,0:T(8,128)(2,1)S(1)} %get-tuple-element.14), channel_id=1, source_target_pairs={{0,2},{1,3},{2,0},{3,1},{4,6},{5,7},{6,4},{7,5},{8,10},{9,11},{10,... | collective-permute-start | bytes 417800 | tf_op jit(solution)/shard_map/ppermute | solution.py:235
  29.1 10.3 %copy-start.5 = (s32[4]{0:T(128)S(1)}, s32[4]{0:T(128)}, u32[]{:S(2)}) copy-start(s32[4]{0:T(128)} %order.1) | copy-start | bytes 52
  29.1 10.3 %collective-permute-start.7 = (s16[2,272,128]{2,1,0:T(8,128)(2,1)S(1)}, s16[2,272,128]{2,1,0:T(8,128)(2,1)S(1)}, u32[]{:S(2)}, u32[]{:S(2)}) collective-permute-start(s16[2,272,128]{2,1,0:T(8,128)(2,1)S(1)} %get-tuple-element.15), channel_id=1, source_target_pairs={{0,3},{1,2},{2,1},{3,0},{4,7},{5,6},{6,5},{7,4},{8,11},{9,10},{10,... | collective-permute-start | bytes 417800 | tf_op jit(solution)/shard_map/ppermute | solution.py:235
  40.2 1.9 %collective-permute-start.8 = (s16[272,128]{1,0:T(8,128)(2,1)S(1)}, s16[272,128]{1,0:T(8,128)(2,1)S(1)}, u32[]{:S(2)}, u32[]{:S(2)}) collective-permute-start(s16[272,128]{1,0:T(8,128)(2,1)S(1)} %get-tuple-element.17), channel_id=1, source_target_pairs={{0,4},{4,0},{8,12},{12,8},{1,5},{5,1},{9,13},{13,9},{2,6},{6,2},{1... | collective-permute-start | bytes 208904 | tf_op jit(solution)/shard_map/ppermute | solution.py:235
  40.3 5.1 %collective-permute-start.9 = (s16[272,128]{1,0:T(8,128)(2,1)S(1)}, s16[272,128]{1,0:T(8,128)(2,1)S(1)}, u32[]{:S(2)}, u32[]{:S(2)}) collective-permute-start(s16[272,128]{1,0:T(8,128)(2,1)S(1)} %get-tuple-element.18), channel_id=1, source_target_pairs={{0,8},{4,12},{8,0},{12,4},{1,9},{5,13},{9,1},{13,5},{2,10},{6,14},... | collective-permute-start | bytes 208904 | tf_op jit(solution)/shard_map/ppermute | solution.py:235
  40.4 5.5 %collective-permute-start.10 = (s16[272,128]{1,0:T(8,128)(2,1)S(1)}, s16[272,128]{1,0:T(8,128)(2,1)S(1)}, u32[]{:S(2)}, u32[]{:S(2)}) collective-permute-start(s16[272,128]{1,0:T(8,128)(2,1)S(1)} %get-tuple-element.19), channel_id=1, source_target_pairs={{0,12},{4,8},{8,4},{12,0},{1,13},{5,9},{9,5},{13,1},{2,14},{6,10},... | collective-permute-start | bytes 208904 | tf_op jit(solution)/shard_map/ppermute | solution.py:235
  46.0 6.5 %collective-permute-start.13 = (s16[272,128]{1,0:T(8,128)(2,1)S(1)}, s16[272,128]{1,0:T(8,128)(2,1)S(1)}, u32[]{:S(2)}, u32[]{:S(2)}) collective-permute-start(s16[272,128]{1,0:T(8,128)(2,1)S(1)} %gather.1.refs_0_), channel_id=1, source_target_pairs={{0,3},{1,2},{2,1},{3,0},{4,7},{5,6},{6,5},{7,4},{8,11},{9,10},{10,... | collective-permute-start | bytes 208904 | tf_op jit(solution)/shard_map/ppermute | solution.py:235
  48.3 8.1 %collective-permute-start.12 = (s16[272,128]{1,0:T(8,128)(2,1)S(1)}, s16[272,128]{1,0:T(8,128)(2,1)S(1)}, u32[]{:S(2)}, u32[]{:S(2)}) collective-permute-start(s16[272,128]{1,0:T(8,128)(2,1)S(1)} %gather.1.refs_0_), channel_id=1, source_target_pairs={{0,2},{1,3},{2,0},{3,1},{4,6},{5,7},{6,4},{7,5},{8,10},{9,11},{10,... | collective-permute-start | bytes 208904 | tf_op jit(solution)/shard_map/ppermute | solution.py:235
  49.5 6.9 %collective-permute-start.11 = (s16[272,128]{1,0:T(8,128)(2,1)S(1)}, s16[272,128]{1,0:T(8,128)(2,1)S(1)}, u32[]{:S(2)}, u32[]{:S(2)}) collective-permute-start(s16[272,128]{1,0:T(8,128)(2,1)S(1)} %gather.1.refs_0_), channel_id=1, source_target_pairs={{0,1},{1,0},{2,3},{3,2},{4,5},{5,4},{6,7},{7,6},{8,9},{9,8},{10,11... | collective-permute-start | bytes 208904 | tf_op jit(solution)/shard_map/ppermute | solution.py:235
where the time goes:
time: 57 us; the launch traced here: 57.5 us
  waiting for transfers between devices  25.4 us (45%)
  starting transfers between devices  15.6 us (27%)
  Pallas kernels  11.2 us (20%)
  local copies, waits for them, and re-layouts  3.23 us (6%)
  between operations  1.38 us (2%)
  other arithmetic  0.69 us (1%)
    ppermute x14, waiting for transfers between devices, over(): return lambda a: lax.ppermute(a, axis, [(i, i ^ mask) for i in range(size)])  25.4 us
    ppermute x14, starting transfers between devices, over(): return lambda a: lax.ppermute(a, axis, [(i, i ^ mask) for i in range(size)])  15.6 us
    pallas_call x2, Pallas kernels, flash(): pl.pallas_call(functools.partial(flash_kernel, tile=tile, chunk=min(tile,...  9.22 us
    unnamed x14, local copies, waits for them, and re-layouts  3.23 us
  transfers between devices with their start and end apart: 14, of which 8 were waited for; matrix products, arithmetic and copies ran while one was open for 1% of the time, Pallas kernels for 6%

commit v1 on v0

--- a/solution.py
+++ b/solution.py
@@ -21,7 +21,6 @@
 TILE_ITEMS = 1536
 VMEM = pl.BlockSpec(memory_space=pltpu.VMEM)
 SMEM = pl.BlockSpec(memory_space=pltpu.SMEM)
-ANY = pl.BlockSpec(memory_space=pl.ANY)
 
 
 def resident(a):
@@ -66,16 +65,16 @@
 def flash_kernel(*refs, tile, chunk, scale, n_before):
     refs = list(refs)
     take = lambda count: [refs.pop(0) for _ in range(count)]
-    query_ref, range_ref = take(2)
+    asked_ref = take(1)[0]
     sources = [take(3) for _ in range(2)]
-    take(1)
     before = take(n_before or 0)
     score_ref, acc, *coded_refs = refs[-3:] if n_before is not None else (refs[-2], refs[-1], refs[0])
     outs = refs[:-3] if n_before is not None else []
     coded_ref = coded_refs[0]
     n, width = sources[0][1].shape
-    rows = query_ref.shape[0]
     lanes = score_ref.shape[1]
+    blocks = asked_ref.shape[0] // (width + STATS)
+    rows = blocks * lanes
     n_split = lax.axis_size("split")
     bank, split = lax.axis_index("bank"), lax.axis_index("split")
     sub = lax.broadcasted_iota(jnp.int32, (8, lanes), 0)
@@ -83,8 +82,10 @@
     @pl.loop(0, rows // lanes)
     def _(half):
         across = pl.ds(pl.multiple_of(half * lanes, lanes), lanes)
-        query = query_ref[across, :]
-        start, end = range_ref[0:1, across], range_ref[1:2, across]
+        query = asked_ref[across, :]
+        code = asked_ref[pl.ds(pl.multiple_of(rows + half * STATS, STATS), STATS), :].astype(jnp.float32)
+        start = (code[2:3] * 4096 + code[1:2] * 64 + code[0:1]).astype(jnp.int32)
+        end = (code[5:6] * 4096 + code[4:5] * 64 + code[3:4]).astype(jnp.int32)
         lowest, highest = jnp.min(start), jnp.max(end)
         length = (end - start) + jnp.int32(MIN32)
         peak = jnp.full((1, lanes), LOW, jnp.float32)
@@ -155,10 +156,10 @@
                     out[g] = whole[:, u * per:(u + 1) * per].astype(jnp.int16)
 
 
-def flash(query, ranges, sources, after, before, scale, n_split):
+def flash(asked, sources, before, scale, n_split):
     n, width = sources[0][1].shape
-    rows = query.shape[0]
-    lanes = min(256, rows)
+    lanes = width
+    rows = asked.shape[0] // (width + STATS) * lanes
     tile = TILE_ITEMS if n % TILE_ITEMS == 0 else 128
     coded = pltpu.VMEM((rows // LANES, width + STATS, LANES), jnp.int16)
     scratch = [pltpu.VMEM((2 * n, lanes), jnp.float32), pltpu.VMEM((width, lanes), jnp.float32)]
@@ -172,15 +173,55 @@
             n_before=None if before is None else len(before),
         ),
         out_shape=out_shape,
-        in_specs=[VMEM] * 2 + [SMEM, VMEM, VMEM] * 2 + [ANY] + [VMEM] * len(before or ()),
+        in_specs=[VMEM] + [SMEM, VMEM, VMEM] * 2 + [VMEM] * len(before or ()),
         out_specs=VMEM if before is None else [VMEM] * n_split,
         scratch_shapes=scratch,
         compiler_params=pltpu.CompilerParams(vmem_limit_bytes=16 << 20),
         name="flash",
     )(
-        resident(query), resident(ranges), *[b for f, k, v in sources for b in (f, resident(k), resident(v))], after,
+        resident(asked), *[b for f, k, v in sources for b in (f, resident(k), resident(v))],
         *map(resident, before or ()),
     )
+
+
+def load_kernel(query, start, end, key, value, asked, key_out, value_out, start_ref, end_ref, sem):
+    rows, width = query.shape
+    pairs = (
+        (start, start_ref), (end, end_ref), (query, asked.at[pl.ds(0, rows)]), (key, key_out), (value, value_out)
+    )
+    copies = [pltpu.make_async_copy(a, b, sem.at[i]) for i, (a, b) in enumerate(pairs)]
+    for copy in copies:
+        copy.start()
+    for copy in copies[:2]:
+        copy.wait()
+    row = lax.broadcasted_iota(jnp.int32, (STATS, width), 0)
+    for half in range(rows // width):
+        across = pl.ds(half * width, width)
+        code = jnp.zeros((STATS, width), jnp.int32)
+        for at, ref in ((0, start_ref), (3, end_ref)):
+            bound = ref[:, across]
+            for digit in range(3):
+                code = jnp.where(row == at + digit, (bound >> (6 * digit)) & 63, code)
+        asked[pl.ds(rows + half * STATS, STATS), :] = code.astype(jnp.float32).astype(jnp.bfloat16)
+    for copy in copies[2:]:
+        copy.wait()
+
+
+def loaded(query, start, end, key, value):
+    rows, width = query.shape
+    arrays = (query, start.reshape(1, rows), end.reshape(1, rows), key, value)
+    return pl.pallas_call(
+        load_kernel,
+        out_shape=[
+            pltpu.VMEM((rows + rows // width * STATS, width), query.dtype),
+            pltpu.VMEM(key.shape, key.dtype), pltpu.VMEM(value.shape, value.dtype),
+        ],
+        in_specs=[pl.BlockSpec(memory_space=pltpu.HBM)] * 5,
+        out_specs=[VMEM] * 3,
+        scratch_shapes=[pltpu.VMEM((1, rows), jnp.int32)] * 2 + [pltpu.SemaphoreType.DMA((5,))],
+        compiler_params=pltpu.CompilerParams(vmem_limit_bytes=16 << 20),
+        name="load",
+    )(*[pltpu.with_memory_space_constraint(a, pltpu.HBM) for a in arrays])
 
 
 def spread_kernel(order, *refs, n_bank, width):
@@ -234,15 +275,14 @@
         size = lax.axis_size(axis)
         return lambda a: lax.ppermute(a, axis, [(i, i ^ mask) for i in range(size)])
 
-    ranges = jnp.stack([range_start, range_end])
-    own = (floor_index, keys, values)
-    partner = tuple(over("bank", 1)(a) for a in own)
-    asked = [(over("bank", 2 * g)(queries), over("bank", 2 * g)(ranges)) for g in range(1, n_bank // 2)]
+    partner = tuple(over("bank", 1)(a) for a in (floor_index, keys, values))
+    mine, own_keys, own_values = loaded(queries, range_start, range_end, keys, values)
+    asked = [mine] + [over("bank", 2 * g)(mine) for g in range(1, n_bank // 2)]
+    sources = [(floor_index, own_keys, own_values), partner]
     coded = []
-    for number, (q, r) in enumerate([(queries, ranges)] + asked):
-        before = coded if number == len(asked) else None
-        result = flash(q, r, [own, partner], asked[0][1], before, scale, n_split)
-        coded.append(result)
+    for number, block in enumerate(asked):
+        before = coded if number == len(asked) - 1 else None
+        coded.append(flash(block, sources, before, scale, n_split))
     messages = coded[-1]
     parts = [messages[0]] + [over("split", k)(messages[k]) for k in range(1, n_split)]
     packed = pltpu.VMEM((width + STATS, per), jnp.int16)

time: 57 us -> 51.1 us (0.90); the launches traced: 57.5 us -> 51 us
  waiting for transfers between devices: 25.4 us -> 21.7 us
  local copies, waits for them, and re-layouts: 3.23 us -> 0.01 us
  Pallas kernels: 11.2 us -> 13.4 us
  starting transfers between devices: 15.6 us -> 14.5 us
  other arithmetic: 0.69 us -> 0 us
    ppermute x14 -> x13, waiting for transfers between devices: 25.4 us -> 21.7 us  [over(): return lambda a: lax.ppermute(a, axis, [(i, i ^ mask) for i in range(size)])]
    unnamed x14 -> x2, local copies, waits for them, and re-layouts: 3.23 us -> 0.01 us
    pallas_call x0 -> x1, Pallas kernels: none -> 1.52 us  [loaded(): pl.pallas_call(load_kernel, out_shape=[pltpu.VMEM((rows + rows // width *...]
    ppermute x14 -> x13, starting transfers between devices: 15.6 us -> 14.5 us  [over(): return lambda a: lax.ppermute(a, axis, [(i, i ^ mask) for i in range(size)])]
    pallas_call x2, Pallas kernels: 9.22 us -> 9.95 us  [flash(): pl.pallas_call(functools.partial(flash_kernel, tile=tile, chunk=min(tile,...]
    another operation x1 -> x0, other arithmetic: 0.69 us -> none  [local(): ranges = jnp.stack([range_start, range_end])]
  transfers between devices with their start and end apart: 14 -> 13, of which waited for: 8 -> 8; matrix products, arithmetic and copies ran while one was open for 1% -> 0% of each run, Pallas kernels for 6% -> 12%
where the time goes in v1:
time: 51.1 us; the launch traced here: 51 us
  waiting for transfers between devices  21.7 us (42%)
  starting transfers between devices  14.5 us (28%)
  Pallas kernels  13.4 us (26%)
  between operations  1.34 us (3%)
    ppermute x13, waiting for transfers between devices, over(): return lambda a: lax.ppermute(a, axis, [(i, i ^ mask) for i in range(size)])  21.7 us
    ppermute x13, starting transfers between devices, over(): return lambda a: lax.ppermute(a, axis, [(i, i ^ mask) for i in range(size)])  14.5 us
    pallas_call x2, Pallas kernels, flash(): pl.pallas_call(functools.partial(flash_kernel, tile=tile, chunk=min(tile,...  9.95 us
    pallas_call x1, Pallas kernels, loaded(): pl.pallas_call(load_kernel, out_shape=[pltpu.VMEM((rows + rows // width *...  1.52 us
  transfers between devices with their start and end apart: 13, of which 8 were waited for; matrix products, arithmetic and copies ran while one was open for 0% of the time, Pallas kernels for 12%

profile of v1, /device:TPU:0, one launch (start us, length us, event | category | flops | bytes accessed | tf_op | source)
XLA Modules:
  0.0 51.0 jit_solution(3890234372736745890)
XLA Ops:
  0.6 0.6 %collective-permute-start.2 = (bf16[1536,256]{1,0:T(8,128)(2,1)}, bf16[1536,256]{1,0:T(8,128)(2,1)S(1)}, u32[]{:S(2)}, u32[]{:S(2)}) collective-permute-start(bf16[1536,256]{1,0:T(8,128)(2,1)} %key.1), channel_id=1, source_target_pairs={{0,4},{4,0},{8,12},{12,8},{1,5},{5,1},{9,13},{13,9},{2,6},{6,2},{1... | collective-permute-start | bytes 2359304 | tf_op jit(solution)/shard_map/ppermute | solution.py:276
  1.2 0.1 collective-permute-start.3
  1.3 1.5 %load.1 = (bf16[544,256]{1,0:T(8,128)(2,1)S(1)}, bf16[1536,256]{1,0:T(8,128)(2,1)S(1)}, bf16[1536,256]{1,0:T(8,128)(2,1)S(1)}) custom-call(bf16[512,256]{1,0:T(8,128)(2,1)} %query.1, s32[1,512]{1,0:T(1,128)} %bitcast.3, s32[1,512]{1,0:T(1,128)} %bitcast.4, bf16[1536,256]{1,0:T(8,128)(2,1)} %key.1, bf16[1536,256]{1,0:T(8,128)(2,1)} %value.1), custom_call_target="tpu_custom_call" | custom-call | tf_op jit(solution)/shard_map/load/pallas_call | solution.py:213
  2.8 3.0 %collective-permute-start = (bf16[544,256]{1,0:T(8,128)(2,1)S(1)}, bf16[544,256]{1,0:T(8,128)(2,1)S(1)}, u32[]{:S(2)}, u32[]{:S(2)}) collective-permute-start(bf16[544,256]{1,0:T(8,128)(2,1)S(1)} %get-tuple-element.15.refs_0_), channel_id=1, source_target_pairs={{0,8},{4,12},{8,0},{12,4},{1,9},{5,13},{9,1},{13,5},{2,10},{6,14},... | collective-permute-start | bytes 835592 | tf_op jit(solution)/shard_map/ppermute | solution.py:276
  5.8 0.0 collective-permute-start.1
  6.4 0.8 %collective-permute-done.1.refs_4_ = s32[1]{0:T(128)} collective-permute-done((s32[1]{0:T(128)}, s32[1]{0:T(128)}, u32[]{:S(2)}, u32[]{:S(2)}) %collective-permute-start.1) | collective-permute-done | bytes 36 | tf_op jit(solution)/shard_map/ppermute | solution.py:276
  7.2 0.0 collective-permute-done.2.refs_5_
  7.2 0.0 collective-permute-done.3.refs_6_
  7.2 4.4 %flash.2.refs_7_ = s16[4,272,128]{2,1,0:T(8,128)(2,1)S(1)} custom-call(bf16[544,256]{1,0:T(8,128)(2,1)S(1)} %get-tuple-element.15.refs_0_, s32[1]{0:T(128)S(6)} %copy.9.refs_1_, bf16[1536,256]{1,0:T(8,128)(2,1)S(1)} %get-tuple-element.16.refs_2_, bf16[1536,256]{1,0:T(8,128)(2,1)S(1)} %get-tuple-element.17.refs_3_, s32[1]{0:T(128)} %collective-permute-done.1.refs_4_, ...), custom_call_target="tpu_custom_call" | custom-call | tf_op jit(solution)/shard_map/flash/pallas_call | solution.py:170
  11.6 1.0 %collective-permute-done.refs_0_ = bf16[544,256]{1,0:T(8,128)(2,1)S(1)} collective-permute-done((bf16[544,256]{1,0:T(8,128)(2,1)S(1)}, bf16[544,256]{1,0:T(8,128)(2,1)S(1)}, u32[]{:S(2)}, u32[]{:S(2)}) %collective-permute-start) | collective-permute-done | bytes 278560 | tf_op jit(solution)/shard_map/ppermute | solution.py:276
  12.7 5.5 %flash.3 = (s16[2,272,128]{2,1,0:T(8,128)(2,1)S(1)}, s16[2,272,128]{2,1,0:T(8,128)(2,1)S(1)}, s16[2,272,128]{2,1,0:T(8,128)(2,1)S(1)}, s16[2,272,128]{2,1,0:T(8,128)(2,1)S(1)}) custom-call(bf16[544,256]{1,0:T(8,128)(2,1)S(1)} %collective-permute-done.refs_0_, s32[1]{0:T(128)S(6)} %copy.9.refs_1_, bf16[1536,256]{1,0:T(8,128)(2,1)S(1)} %get-tuple-element.16.refs_2_, ...), custom_call_target="tpu_custom_call" | custom-call | tf_op jit(solution)/shard_map/flash/pallas_call | solution.py:170
  18.2 1.9 %collective-permute-start.4 = (s16[2,272,128]{2,1,0:T(8,128)(2,1)S(1)}, s16[2,272,128]{2,1,0:T(8,128)(2,1)S(1)}, u32[]{:S(2)}, u32[]{:S(2)}) collective-permute-start(s16[2,272,128]{2,1,0:T(8,128)(2,1)S(1)} %get-tuple-element.19), channel_id=1, source_target_pairs={{0,1},{1,0},{2,3},{3,2},{4,5},{5,4},{6,7},{7,6},{8,9},{9,8},{10,11... | collective-permute-start | bytes 417800 | tf_op jit(solution)/shard_map/ppermute | solution.py:276
  20.1 2.6 %collective-permute-start.5 = (s16[2,272,128]{2,1,0:T(8,128)(2,1)S(1)}, s16[2,272,128]{2,1,0:T(8,128)(2,1)S(1)}, u32[]{:S(2)}, u32[]{:S(2)}) collective-permute-start(s16[2,272,128]{2,1,0:T(8,128)(2,1)S(1)} %get-tuple-element.20), channel_id=1, source_target_pairs={{0,2},{1,3},{2,0},{3,1},{4,6},{5,7},{6,4},{7,5},{8,10},{9,11},{10,... | collective-permute-start | bytes 417800 | tf_op jit(solution)/shard_map/ppermute | solution.py:276
  22.7 0.0 copy-start
  22.7 0.0 collective-permute-start.6
  22.7 2.2 %collective-permute-done.4.refs_1_ = s16[2,272,128]{2,1,0:T(8,128)(2,1)S(1)} collective-permute-done((s16[2,272,128]{2,1,0:T(8,128)(2,1)S(1)}, s16[2,272,128]{2,1,0:T(8,128)(2,1)S(1)}, u32[]{:S(2)}, u32[]{:S(2)}) %collective-permute-start.4) | collective-permute-done | bytes 139296 | tf_op jit(solution)/shard_map/ppermute | solution.py:276
  24.9 7.7 %collective-permute-done.5.refs_2_ = s16[2,272,128]{2,1,0:T(8,128)(2,1)S(1)} collective-permute-done((s16[2,272,128]{2,1,0:T(8,128)(2,1)S(1)}, s16[2,272,128]{2,1,0:T(8,128)(2,1)S(1)}, u32[]{:S(2)}, u32[]{:S(2)}) %collective-permute-start.5) | collective-permute-done | bytes 139296 | tf_op jit(solution)/shard_map/ppermute | solution.py:276
  32.6 0.0 collective-permute-done.6.refs_3_
  32.6 0.0 copy-done
  32.6 0.8 %spread.1 = (s16[272,128]{1,0:T(8,128)(2,1)S(1)}, s16[272,128]{1,0:T(8,128)(2,1)S(1)}, s16[272,128]{1,0:T(8,128)(2,1)S(1)}, s16[272,128]{1,0:T(8,128)(2,1)S(1)}) custom-call(s32[4]{0:T(128)S(1)} %copy-done, s16[2,272,128]{2,1,0:T(8,128)(2,1)S(1)} %get-tuple-element.18.refs_0_, s16[2,272,128]{2,1,0:T(8,128)(2,1)S(1)} %collective-permute-done.4.refs_1_, ...), custom_call_target="tpu_custom_call" | custom-call | tf_op jit(solution)/shard_map/spread/pallas_call | solution.py:289
  33.5 0.1 collective-permute-start.7
  33.5 0.3 collective-permute-start.8
  33.9 1.5 %collective-permute-start.9 = (s16[272,128]{1,0:T(8,128)(2,1)S(1)}, s16[272,128]{1,0:T(8,128)(2,1)S(1)}, u32[]{:S(2)}, u32[]{:S(2)}) collective-permute-start(s16[272,128]{1,0:T(8,128)(2,1)S(1)} %get-tuple-element.25), channel_id=1, source_target_pairs={{0,12},{4,8},{8,4},{12,0},{1,13},{5,9},{9,5},{13,1},{2,14},{6,10},... | collective-permute-start | bytes 208904 | tf_op jit(solution)/shard_map/ppermute | solution.py:276
  35.4 0.0 collective-permute-done.7.refs_1_
  35.4 3.3 %collective-permute-done.8.refs_2_ = s16[272,128]{1,0:T(8,128)(2,1)S(1)} collective-permute-done((s16[272,128]{1,0:T(8,128)(2,1)S(1)}, s16[272,128]{1,0:T(8,128)(2,1)S(1)}, u32[]{:S(2)}, u32[]{:S(2)}) %collective-permute-start.8) | collective-permute-done | bytes 69664 | tf_op jit(solution)/shard_map/ppermute | solution.py:276
  38.7 0.4 collective-permute-done.9.refs_3_
  39.1 0.1 gather.1.refs_0_
  39.2 2.6 %collective-permute-start.12 = (s16[272,128]{1,0:T(8,128)(2,1)S(1)}, s16[272,128]{1,0:T(8,128)(2,1)S(1)}, u32[]{:S(2)}, u32[]{:S(2)}) collective-permute-start(s16[272,128]{1,0:T(8,128)(2,1)S(1)} %gather.1.refs_0_), channel_id=1, source_target_pairs={{0,3},{1,2},{2,1},{3,0},{4,7},{5,6},{6,5},{7,4},{8,11},{9,10},{10,... | collective-permute-start | bytes 208904 | tf_op jit(solution)/shard_map/ppermute | solution.py:276
  41.8 1.5 %collective-permute-start.11 = (s16[272,128]{1,0:T(8,128)(2,1)S(1)}, s16[272,128]{1,0:T(8,128)(2,1)S(1)}, u32[]{:S(2)}, u32[]{:S(2)}) collective-permute-start(s16[272,128]{1,0:T(8,128)(2,1)S(1)} %gather.1.refs_0_), channel_id=1, source_target_pairs={{0,2},{1,3},{2,0},{3,1},{4,6},{5,7},{6,4},{7,5},{8,10},{9,11},{10,... | collective-permute-start | bytes 208904 | tf_op jit(solution)/shard_map/ppermute | solution.py:276
  43.3 0.4 collective-permute-start.10
  43.7 2.0 %collective-permute-done.12.refs_3_ = s16[272,128]{1,0:T(8,128)(2,1)S(1)} collective-permute-done((s16[272,128]{1,0:T(8,128)(2,1)S(1)}, s16[272,128]{1,0:T(8,128)(2,1)S(1)}, u32[]{:S(2)}, u32[]{:S(2)}) %collective-permute-start.12) | collective-permute-done | bytes 69664 | tf_op jit(solution)/shard_map/ppermute | solution.py:276
  45.6 4.3 %collective-permute-done.11.refs_2_ = s16[272,128]{1,0:T(8,128)(2,1)S(1)} collective-permute-done((s16[272,128]{1,0:T(8,128)(2,1)S(1)}, s16[272,128]{1,0:T(8,128)(2,1)S(1)}, u32[]{:S(2)}, u32[]{:S(2)}) %collective-permute-start.11) | collective-permute-done | bytes 69664 | tf_op jit(solution)/shard_map/ppermute | solution.py:276
  49.9 0.0 collective-permute-done.10.refs_1_
  49.9 1.0 %final.1 = (f32[512,256]{1,0:T(8,128)}, f32[4,128]{1,0:T(4,128)}) custom-call(s16[272,128]{1,0:T(8,128)(2,1)S(1)} %gather.1.refs_0_, s16[272,128]{1,0:T(8,128)(2,1)S(1)} %collective-permute-done.10.refs_1_, s16[272,128]{1,0:T(8,128)(2,1)S(1)} %collective-permute-done.11.refs_2_, s16[272,128]{1,0:T(8,128)(2,1)S(1)} %collective-permute-done.12.refs_3_), custom_call_target="tpu_custom_call" | custom-call | tf_op jit(solution)/shard_map/final/pallas_call | solution.py:308
Async XLA Ops:
  0.6 6.6 %collective-permute-start.2 = (bf16[1536,256]{1,0:T(8,128)(2,1)}, bf16[1536,256]{1,0:T(8,128)(2,1)S(1)}, u32[]{:S(2)}, u32[]{:S(2)}) collective-permute-start(bf16[1536,256]{1,0:T(8,128)(2,1)} %key.1), channel_id=1, source_target_pairs={{0,4},{4,0},{8,12},{12,8},{1,5},{5,1},{9,13},{13,9},{2,6},{6,2},{1... | collective-permute-start | bytes 2359304 | tf_op jit(solution)/shard_map/ppermute | solution.py:276
  1.2 6.0 %collective-permute-start.3 = (bf16[1536,256]{1,0:T(8,128)(2,1)}, bf16[1536,256]{1,0:T(8,128)(2,1)S(1)}, u32[]{:S(2)}, u32[]{:S(2)}) collective-permute-start(bf16[1536,256]{1,0:T(8,128)(2,1)} %value.1), channel_id=1, source_target_pairs={{0,4},{4,0},{8,12},{12,8},{1,5},{5,1},{9,13},{13,9},{2,6},{6,2},{1... | collective-permute-start | bytes 2359304 | tf_op jit(solution)/shard_map/ppermute | solution.py:276
  2.8 9.9 %collective-permute-start = (bf16[544,256]{1,0:T(8,128)(2,1)S(1)}, bf16[544,256]{1,0:T(8,128)(2,1)S(1)}, u32[]{:S(2)}, u32[]{:S(2)}) collective-permute-start(bf16[544,256]{1,0:T(8,128)(2,1)S(1)} %get-tuple-element.15.refs_0_), channel_id=1, source_target_pairs={{0,8},{4,12},{8,0},{12,4},{1,9},{5,13},{9,1},{13,5},{2,10},{6,14},... | collective-permute-start | bytes 835592 | tf_op jit(solution)/shard_map/ppermute | solution.py:276
  5.8 1.4 %collective-permute-start.1 = (s32[1]{0:T(128)}, s32[1]{0:T(128)}, u32[]{:S(2)}, u32[]{:S(2)}) collective-permute-start(s32[1]{0:T(128)} %param.12), channel_id=1, source_target_pairs={{0,4},{4,0},{8,12},{12,8},{1,5},{5,1},{9,13},{13,9},{2,6},{6,2},{1... | collective-permute-start | bytes 20 | tf_op jit(solution)/shard_map/ppermute | solution.py:276
  18.2 6.7 %collective-permute-start.4 = (s16[2,272,128]{2,1,0:T(8,128)(2,1)S(1)}, s16[2,272,128]{2,1,0:T(8,128)(2,1)S(1)}, u32[]{:S(2)}, u32[]{:S(2)}) collective-permute-start(s16[2,272,128]{2,1,0:T(8,128)(2,1)S(1)} %get-tuple-element.19), channel_id=1, source_target_pairs={{0,1},{1,0},{2,3},{3,2},{4,5},{5,4},{6,7},{7,6},{8,9},{9,8},{10,11... | collective-permute-start | bytes 417800 | tf_op jit(solution)/shard_map/ppermute | solution.py:276
  20.1 12.5 %collective-permute-start.5 = (s16[2,272,128]{2,1,0:T(8,128)(2,1)S(1)}, s16[2,272,128]{2,1,0:T(8,128)(2,1)S(1)}, u32[]{:S(2)}, u32[]{:S(2)}) collective-permute-start(s16[2,272,128]{2,1,0:T(8,128)(2,1)S(1)} %get-tuple-element.20), channel_id=1, source_target_pairs={{0,2},{1,3},{2,0},{3,1},{4,6},{5,7},{6,4},{7,5},{8,10},{9,11},{10,... | collective-permute-start | bytes 417800 | tf_op jit(solution)/shard_map/ppermute | solution.py:276
  22.7 10.0 %copy-start = (s32[4]{0:T(128)S(1)}, s32[4]{0:T(128)}, u32[]{:S(2)}) copy-start(s32[4]{0:T(128)} %order.1) | copy-start | bytes 52
  22.7 10.0 %collective-permute-start.6 = (s16[2,272,128]{2,1,0:T(8,128)(2,1)S(1)}, s16[2,272,128]{2,1,0:T(8,128)(2,1)S(1)}, u32[]{:S(2)}, u32[]{:S(2)}) collective-permute-start(s16[2,272,128]{2,1,0:T(8,128)(2,1)S(1)} %get-tuple-element.21), channel_id=1, source_target_pairs={{0,3},{1,2},{2,1},{3,0},{4,7},{5,6},{6,5},{7,4},{8,11},{9,10},{10,... | collective-permute-start | bytes 417800 | tf_op jit(solution)/shard_map/ppermute | solution.py:276
  33.5 1.9 %collective-permute-start.7 = (s16[272,128]{1,0:T(8,128)(2,1)S(1)}, s16[272,128]{1,0:T(8,128)(2,1)S(1)}, u32[]{:S(2)}, u32[]{:S(2)}) collective-permute-start(s16[272,128]{1,0:T(8,128)(2,1)S(1)} %get-tuple-element.23), channel_id=1, source_target_pairs={{0,4},{4,0},{8,12},{12,8},{1,5},{5,1},{9,13},{13,9},{2,6},{6,2},{1... | collective-permute-start | bytes 208904 | tf_op jit(solution)/shard_map/ppermute | solution.py:276
  33.5 5.1 %collective-permute-start.8 = (s16[272,128]{1,0:T(8,128)(2,1)S(1)}, s16[272,128]{1,0:T(8,128)(2,1)S(1)}, u32[]{:S(2)}, u32[]{:S(2)}) collective-permute-start(s16[272,128]{1,0:T(8,128)(2,1)S(1)} %get-tuple-element.24), channel_id=1, source_target_pairs={{0,8},{4,12},{8,0},{12,4},{1,9},{5,13},{9,1},{13,5},{2,10},{6,14},... | collective-permute-start | bytes 208904 | tf_op jit(solution)/shard_map/ppermute | solution.py:276
  33.9 5.2 %collective-permute-start.9 = (s16[272,128]{1,0:T(8,128)(2,1)S(1)}, s16[272,128]{1,0:T(8,128)(2,1)S(1)}, u32[]{:S(2)}, u32[]{:S(2)}) collective-permute-start(s16[272,128]{1,0:T(8,128)(2,1)S(1)} %get-tuple-element.25), channel_id=1, source_target_pairs={{0,12},{4,8},{8,4},{12,0},{1,13},{5,9},{9,5},{13,1},{2,14},{6,10},... | collective-permute-start | bytes 208904 | tf_op jit(solution)/shard_map/ppermute | solution.py:276
  39.2 6.4 %collective-permute-start.12 = (s16[272,128]{1,0:T(8,128)(2,1)S(1)}, s16[272,128]{1,0:T(8,128)(2,1)S(1)}, u32[]{:S(2)}, u32[]{:S(2)}) collective-permute-start(s16[272,128]{1,0:T(8,128)(2,1)S(1)} %gather.1.refs_0_), channel_id=1, source_target_pairs={{0,3},{1,2},{2,1},{3,0},{4,7},{5,6},{6,5},{7,4},{8,11},{9,10},{10,... | collective-permute-start | bytes 208904 | tf_op jit(solution)/shard_map/ppermute | solution.py:276
  41.8 8.1 %collective-permute-start.11 = (s16[272,128]{1,0:T(8,128)(2,1)S(1)}, s16[272,128]{1,0:T(8,128)(2,1)S(1)}, u32[]{:S(2)}, u32[]{:S(2)}) collective-permute-start(s16[272,128]{1,0:T(8,128)(2,1)S(1)} %gather.1.refs_0_), channel_id=1, source_target_pairs={{0,2},{1,3},{2,0},{3,1},{4,6},{5,7},{6,4},{7,5},{8,10},{9,11},{10,... | collective-permute-start | bytes 208904 | tf_op jit(solution)/shard_map/ppermute | solution.py:276
  43.3 6.7 %collective-permute-start.10 = (s16[272,128]{1,0:T(8,128)(2,1)S(1)}, s16[272,128]{1,0:T(8,128)(2,1)S(1)}, u32[]{:S(2)}, u32[]{:S(2)}) collective-permute-start(s16[272,128]{1,0:T(8,128)(2,1)S(1)} %gather.1.refs_0_), channel_id=1, source_target_pairs={{0,1},{1,0},{2,3},{3,2},{4,5},{5,4},{6,7},{7,6},{8,9},{9,8},{10,11... | collective-permute-start | bytes 208904 | tf_op jit(solution)/shard_map/ppermute | solution.py:276
